TPU v7x, 32 devices: a whole 2x2x4 slice. The times are simulated.
32 devices in a mesh: seg: 2 (over y), chan: 8 (over z, core), tm: 2 (over x).
Axes of the slice: x: 2, y: 2, z: 4, core: 2. Of those that a mesh axis runs over, the one named last changes fastest.
Arguments:
- traces: bfloat16 [1024, 12288], P(('seg', 'chan'), 'tm'), parts along dimension 0, may hold values from -14 to 14
- filter_taps: float32 [512, 33], P('chan'), may hold values from -1 to 1
- source_counts: int32 [8], replicated, may hold values from 1 to 36, 96 in all
- source_channel: int32 [8, 36], replicated, may hold values from 0 to 63
- block_sources: int32 [8, 12], P('chan'), may hold values from 0 to 95
Outputs:
- stacked: float32 [1024, 12, 1024], P(('seg', 'chan', 'tm')), parts along dimension 0
There are 2 independent parts, one for each index of `seg`. A program takes and returns all parts, laid end to end along the dimension named above; an argument that names none is the same for every part. Nothing has to cross between parts.
Inputs may be any that keep to these rules, and one draw needn't show every extreme that they name: `source_counts`: the entries sum to 96 and the largest is exactly 36. `source_channel`: only the first source_counts[h] entries of row h name virtual sources.
All inputs are finite; a program needn't handle non-finite values.
Results may differ from a plain program's by a relative error of at most 0.0072.
Values may be sent and summed in bfloat16 or wider, within the bound.
No kernel may reach another device: no remote copies, remote signals or barrier semaphores. Data moves between devices by JAX's collectives and lax.ppermute only.
A program may use at most 64 MiB of HBM per device.

v0:
```python
import math
import jax
import jax.numpy as jnp
from jax import lax
from jax.sharding import PartitionSpec as P

TILE = 64
NFFT = 4096
NF = 512
F0 = 8


def from_behind(block, axis, distance):
    devices = range(lax.axis_size(axis))
    route = [(i - distance, i) for i in devices if i - distance in devices]
    return lax.ppermute(block, axis, route)


def transform_table():
    sample_index = jnp.arange(NFFT, dtype=jnp.int32)[:, None]
    frequency = F0 + jnp.arange(NF, dtype=jnp.int32)[None, :]
    phase_index = frequency * sample_index % NFFT
    angles = phase_index.astype(jnp.float32) * jnp.float32(2.0 * math.pi / NFFT)
    cosine = jnp.cos(angles).astype(jnp.bfloat16)
    sine_part = (-jnp.sin(angles)).astype(jnp.bfloat16)
    return jnp.concatenate([cosine, sine_part], axis=1)


def apply_filter(extended, filter_taps):
    tap_count = filter_taps.shape[1]
    length = extended.shape[1] - (tap_count - 1)
    summed = jnp.zeros((extended.shape[0], length), jnp.float32)
    for tap_index in range(tap_count):
        first_sample = tap_count - 1 - tap_index
        summed = (
            summed
            + filter_taps[:, tap_index : tap_index + 1]
            * extended[:, first_sample : first_sample + length]
        )
    return summed.astype(jnp.bfloat16)


def intersecting(filtered, hop_length):
    channel_count = filtered.shape[0]
    pieces = filtered.reshape(channel_count, -1, hop_length)
    return jnp.concatenate([pieces[:, :-1], pieces[:, 1:]], axis=2)


def whiten(spectra):
    half_width = spectra.shape[-1] // 2
    real_part = spectra[..., :half_width]
    imag_part = spectra[..., half_width:]
    powers = real_part * real_part + imag_part * imag_part
    widths = [(0, 0)] * (powers.ndim - 1) + [(2, 2)]
    padded = jnp.pad(powers, widths)
    smooth = (
        padded[..., 0:half_width]
        + padded[..., 1 : half_width + 1]
        + padded[..., 2 : half_width + 2]
        + padded[..., 3 : half_width + 3]
        + padded[..., 4 : half_width + 4]
    ) / 5.0
    mean_power = jnp.mean(powers, axis=-1, keepdims=True)
    scaling = lax.rsqrt(smooth + 0.1 * mean_power + 1e-06)
    return jnp.concatenate([real_part * scaling, imag_part * scaling], axis=-1).astype(jnp.bfloat16)


def correlate(receivers, sources, factor):
    half_width = receivers.shape[-1] // 2
    receiver_real = receivers[..., :half_width]
    receiver_imag = receivers[..., half_width:]
    source_real = sources[..., :half_width]
    source_imag = sources[..., half_width:]
    real_sum = jnp.sum(source_real * receiver_real + source_imag * receiver_imag, axis=-2)
    imag_sum = jnp.sum(source_real * receiver_imag - source_imag * receiver_real, axis=-2)
    return jnp.concatenate([real_sum, imag_sum], axis=-1) * factor


def source_rows(source_counts, source_channel, wanted):
    offsets = jnp.cumsum(source_counts) - source_counts
    home_group = jnp.sum((wanted[..., None] >= offsets).astype(jnp.int32), axis=-1) - 1
    slot_index = wanted - offsets[home_group]
    local_channel = source_channel[home_group, slot_index]
    return (home_group, slot_index, local_channel)


def shards(traces, filter_taps, source_counts, source_channel, block_sources):
    channels_here, samples_here = traces.shape
    tap_count = filter_taps.shape[1]
    hop_length = NFFT // 2
    halo_width = hop_length + tap_count - 1
    tail_samples = from_behind(traces[:, samples_here - halo_width :], "tm", 1)
    extended = jnp.concatenate([tail_samples, traces], axis=1).astype(jnp.float32)
    filtered = apply_filter(extended, filter_taps)
    windows_here = samples_here // hop_length
    windows = intersecting(filtered, hop_length).reshape(channels_here * windows_here, NFFT)
    spectra = jnp.dot(windows, transform_table(), preferred_element_type=jnp.float32)
    whitened = whiten(spectra).reshape(channels_here, windows_here, 2 * NF)
    home_group, slot_index, local_channel = source_rows(
        source_counts, source_channel, block_sources
    )
    slot_count = source_channel.shape[1]
    group_index = lax.axis_index("chan")
    own_slots = source_channel[group_index]
    slot_rows = whitened[own_slots]
    everything = lax.all_gather(slot_rows, "chan", axis=0, tiled=True)
    picked = everything[home_group * slot_count + slot_index]
    time_groups = lax.axis_size("tm")
    factor = 1.0 / (windows_here * time_groups)
    receivers = whitened.astype(jnp.float32)
    tile_of_row = (
        jnp.arange(channels_here // time_groups * lax.axis_size("tm"), dtype=jnp.int32) // TILE
    )
    sources = picked[tile_of_row].astype(jnp.float32)
    return lax.psum_scatter(
        correlate(receivers[:, None], sources, factor), "tm", scatter_dimension=0, tiled=True
    )


def solution(mesh):
    in_specs = (P(("seg", "chan"), "tm"), P("chan", None), P(), P(), P("chan", None))
    out_specs = P(("seg", "chan", "tm"), None, None)
    return jax.shard_map(shards, mesh=mesh, in_specs=in_specs, out_specs=out_specs, check_vma=False)
```

profile of v0, /device:TPU:0, one launch (start us, length us, event | category | flops | bytes accessed | tf_op | source)
XLA Modules:
  0.0 170.6 jit_solution(2282567406715070541)
XLA Ops:
  6.5 0.0 all-gather.3.cloned.1.call-start
  6.5 1.1 slice.239
  7.6 4.9 %collective-permute-start = (bf16[64,2080]{1,0:T(8,128)(2,1)S(1)}, bf16[64,2080]{1,0:T(8,128)(2,1)S(1)}, u32[]{:S(2)}, u32[]{:S(2)}) collective-permute-start(bf16[64,2080]{1,0:T(8,128)(2,1)S(1)} %slice.239), channel_id=1, source_target_pairs={{0,1},{2,3},{4,5},{6,7},{8,9},{10,11},{12,13},{14,15},{16,17},{18,... | collective-permute-start | bytes 798728 | tf_op jit(solution)/shard_map/ppermute | solution.py:16
  12.5 1.0 slice_bitcast_fusion.33
  13.5 0.0 copy-start
  13.5 35.0 %cosine_convert_fusion = (bf16[4096,512]{1,0:T(8,128)(2,1)}, bf16[4096,512]{1,0:T(8,128)(2,1)}) fusion(s32[512]{0:T(512)S(1)} %iota_add_fusion), kind=kLoop, calls=%fused_computation.14 | loop fusion | flops 35651584 | bytes 8390656 | tf_op jit(solution)/shard_map/convert_element_type | solution.py:24
  48.6 0.7 fusion.51
  49.3 1.0 slice_bitcast_fusion.34
  50.3 0.0 collective-permute-done
  50.3 0.0 copy-done
  50.3 0.3 maximum_convert_fusion
  50.6 18.0 %fusion.11 = bf16[64,8192]{1,0:T(8,128)(2,1)S(1)} fusion(f32[64,8224]{1,0:T(8,128)S(1)} %maximum_convert_fusion, f32[64]{0:T(128)S(1)} %get-tuple-element.48, f32[64]{0:T(128)S(1)} %get-tuple-element.49, f32[64]{0:T(128)S(1)} %get-tuple-element.18, f32[64]{0:T(128)S(1)} %get-tuple-element.19, f32[64]{0:T(128)S(1)} %get-tuple-element.20, ...), kind=kLoop, calls=%fused_computation.23 | loop fusion | flops 34603008 | bytes 70263040 | tf_op jit(solution)/shard_map/convert_element_type | solution.py:40
  68.5 0.8 reshape.253
  69.4 1.3 fusion.58
  70.6 1.5 pad_maximum_fusion
  72.1 2.5 %reshape.254 = bf16[192,4096]{1,0:T(8,128)(2,1)} reshape(bf16[64,3,4096]{2,1,0:T(4,128)(2,1)S(1)} %pad_maximum_fusion) | data formatting | bytes 3145728 | tf_op jit(solution)/shard_map/reshape | solution.py:96
  74.6 5.7 %fusion.3 = f32[192,1024]{1,0:T(8,128)S(1)} fusion(bf16[192,4096]{1,0:T(8,128)(2,1)} %reshape.254, bf16[4096,512]{1,0:T(8,128)(2,1)} %get-tuple-element.51, bf16[4096,512]{1,0:T(8,128)(2,1)} %get-tuple-element.50), kind=kOutput, calls=%fused_computation.9 | convolution fusion | flops 1627389952 | bytes 10747904 | tf_op jit(solution)/shard_map/dot_general | solution.py:97
  80.3 0.1 fusion.57
  80.5 0.5 multiply_convert_fusion.1
  81.0 0.0 copy-start.2
  81.0 0.0 copy-start.1
  81.0 0.1 multiply_convert_fusion
  81.1 0.1 concatenate.39
  81.2 0.1 concatenate.38
  81.3 0.2 pad_maximum_fusion.1
  81.5 1.6 gather_fusion
  83.1 0.0 all-gather.3.cloned.1.call-update
  83.1 0.0 reduce-scatter.2.cloned.1.call-start
  83.2 0.0 copy-done.2
  83.2 0.2 reduce-window.9
  83.4 0.0 copy-done.1
  83.4 0.1 convert_reduce_fusion
  83.5 0.7 gather_fusion.1
  84.2 0.1 concatenate.42
  84.3 0.1 concatenate.41
  84.4 0.3 maximum_convert_fusion.1
  84.7 0.2 slice_bitcast_fusion.1
  84.9 0.1 copy.6
  85.1 0.1 copy.7
  85.2 29.9 %all-gather.3.cloned.1.call-done = bf16[288,3,1024]{2,1,0:T(4,128)(2,1)} async-done(((bf16[36,3,1024]{2,1,0:T(4,128)(2,1)}), bf16[288,3,1024]{2,1,0:T(4,128)(2,1)}) %all-gather.3.cloned.1.call-update) | async-done | bytes 1769488 | tf_op jit(solution)/shard_map/all_gather | solution.py:106
  115.1 2.3 %gather_fusion.2 = bf16[12,3,1024]{2,1,0:T(4,128)(2,1)S(1)} fusion(bf16[288,3,1024]{2,1,0:T(4,128)(2,1)} %all-gather.3.cloned.1.call-done, s32[1024]{0:T(1024)S(1)} %pad_clamp_fusion), kind=kCustom, calls=%fused_computation.2 | custom fusion | bytes 147504 | tf_op jit(solution)/shard_map/gather | solution.py:107
  117.4 1.5 add_reduce_fusion
  118.9 2.1 %maximum_multiply_fusion = f32[64,12,1024]{2,0,1:T(8,128)} fusion(f32[64,12,512]{2,0,1:T(8,128)S(1)} %get-tuple-element.6, f32[64,12,512]{2,0,1:T(8,128)S(1)} %get-tuple-element.5), kind=kLoop, calls=%fused_computation.20 | loop fusion | flops 1572864 | bytes 6291456 | tf_op jit(solution)/shard_map/mul | solution.py:76
  120.9 0.0 reduce-scatter.2.cloned.1.call-update
  121.0 42.8 %reduce-scatter.2.cloned.1.call-done = f32[32,12,1024]{2,0,1:T(8,128)} async-done(((f32[64,12,1024]{2,0,1:T(8,128)}), f32[32,12,1024]{2,0,1:T(8,128)}) %reduce-scatter.2.cloned.1.call-update) | async-done | bytes 1572880 | tf_op jit(solution)/shard_map/reduce_scatter | solution.py:115
  (9 shorter events, 0.1 us)
Async XLA Ops:
  6.5 108.5 %all-gather.3.cloned.1.call-start = ((), (), s32[]{:S(2)}) async-start(), calls=%async_computation.2 | async-start | bytes 2654208 | tf_op jit(solution)/shard_map/all_gather | solution.py:106
  7.6 42.6 %collective-permute-start = (bf16[64,2080]{1,0:T(8,128)(2,1)S(1)}, bf16[64,2080]{1,0:T(8,128)(2,1)S(1)}, u32[]{:S(2)}, u32[]{:S(2)}) collective-permute-start(bf16[64,2080]{1,0:T(8,128)(2,1)S(1)} %slice.239), channel_id=1, source_target_pairs={{0,1},{2,3},{4,5},{6,7},{8,9},{10,11},{12,13},{14,15},{16,17},{18,... | collective-permute-start | bytes 798728 | tf_op jit(solution)/shard_map/ppermute | solution.py:16
  13.5 36.8 %copy-start = (bf16[64,6144]{1,0:T(8,128)(2,1)S(1)}, bf16[64,6144]{1,0:T(8,128)(2,1)}, u32[]{:S(2)}) copy-start(bf16[64,6144]{1,0:T(8,128)(2,1)} %param.5) | copy-start | bytes 2359300
  81.0 2.2 %copy-start.2 = (s32[8]{0:T(128)S(1)}, s32[8]{0:T(128)}, u32[]{:S(2)}) copy-start(s32[8]{0:T(128)} %param.7) | copy-start | bytes 100
  81.0 2.4 %copy-start.1 = (s32[1,12]{1,0:T(1,128)S(1)}, s32[1,12]{1,0:T(1,128)}, u32[]{:S(2)}) copy-start(s32[1,12]{1,0:T(1,128)} %param.9) | copy-start | bytes 148
  83.1 80.7 %reduce-scatter.2.cloned.1.call-start = ((), (), s32[]{:S(2)}) async-start(), calls=%async_computation.1 | async-start | bytes 4718592 | tf_op jit(solution)/shard_map/reduce_scatter | solution.py:115
Sparse Core Ops, SparseCore 0:
  83.3 31.7 all-gather.2
  121.1 42.6 reduce-scatter.1
where the time goes:
time: 171 us
  waiting for transfers between devices  72.8 us (43%)
  other arithmetic  60.5 us (35%)
  between operations  13.6 us (8%)
  local copies, waits for them, and re-layouts  13.1 us (8%)
  matrix products  5.69 us (3%)
  starting transfers between devices  4.93 us (3%)
    reduce_scatter x1, waiting for transfers between devices, shards(): lax.psum_scatter(correlate(receivers[:, None], sources, factor), 'tm', sc...  42.8 us
    convert_element_type x1, other arithmetic, transform_table(): cosine = jnp.cos(angles).astype(jnp.bfloat16)  35 us
    all_gather x1, waiting for transfers between devices, shards(): everything = lax.all_gather(slot_rows, 'chan', axis=0, tiled=True)  29.9 us
    convert_element_type x1, other arithmetic, apply_filter(): return summed.astype(jnp.bfloat16)  18 us
    dot_general x1, matrix products, shards(): jnp.dot(windows, transform_table(), preferred_element_type=jnp.float32)  5.69 us
    ppermute x1, starting transfers between devices, from_behind(): return lax.ppermute(block, axis, route)  4.89 us
  transfers between devices with their start and end apart: 3, of which 2 were waited for; matrix products, arithmetic and copies ran while one was open for 23% of the time, Pallas kernels for 0%

commit v1 on v0

--- a/solution.py
+++ b/solution.py
@@ -103,7 +103,9 @@
     group_index = lax.axis_index("chan")
     own_slots = source_channel[group_index]
     slot_rows = whitened[own_slots]
-    everything = lax.all_gather(slot_rows, "chan", axis=0, tiled=True)
+    everything = jnp.concatenate(
+        lax.all_to_all(jnp.stack([slot_rows] * lax.axis_size("chan")), "chan", 0, 0), axis=0
+    )
     picked = everything[home_group * slot_count + slot_index]
     time_groups = lax.axis_size("tm")
     factor = 1.0 / (windows_here * time_groups)

time: 171 us -> 193 us (1.13)
  waiting for transfers between devices: 72.8 us -> 85.8 us
  starting transfers between devices: 4.93 us -> 9.93 us
  local copies, waits for them, and re-layouts: 13.1 us -> 16.9 us
    all_to_all x0 -> x1, waiting for transfers between devices: none -> 44.2 us  [shards(): lax.all_to_all(jnp.stack([slot_rows] * lax.axis_size('chan')), 'chan', 0, 0)]
    all_gather x1 -> x0, waiting for transfers between devices: 29.9 us -> none  [shards(): everything = lax.all_gather(slot_rows, 'chan', axis=0, tiled=True)]
    all_to_all x0 -> x1, starting transfers between devices: none -> 5.01 us  [shards(): lax.all_to_all(jnp.stack([slot_rows] * lax.axis_size('chan')), 'chan', 0, 0)]
    reshape x0 -> x1, local copies, waits for them, and re-layouts: none -> 2.93 us  [shards(): jnp.concatenate(lax.all_to_all(jnp.stack([slot_rows] * lax.axis_size('cha...]
  transfers between devices with their start and end apart: 3 -> 3, of which waited for: 2 -> 2; matrix products, arithmetic and copies ran while one was open for 23% -> 21% of each run, Pallas kernels for 0% -> 0%
where the time goes in v1:
time: 193 us; the launch traced here: 192 us
  waiting for transfers between devices  85.8 us (44%)
  other arithmetic  60.5 us (31%)
  local copies, waits for them, and re-layouts  16.9 us (9%)
  between operations  13.6 us (7%)
  starting transfers between devices  9.93 us (5%)
  matrix products  5.69 us (3%)
    all_to_all x1, waiting for transfers between devices, shards(): lax.all_to_all(jnp.stack([slot_rows] * lax.axis_size('chan')), 'chan', 0, 0)  44.2 us
    reduce_scatter x1, waiting for transfers between devices, shards(): lax.psum_scatter(correlate(receivers[:, None], sources, factor), 'tm', sc...  41.6 us
    convert_element_type x1, other arithmetic, transform_table(): cosine = jnp.cos(angles).astype(jnp.bfloat16)  35 us
    convert_element_type x1, other arithmetic, apply_filter(): return summed.astype(jnp.bfloat16)  18 us
    dot_general x1, matrix products, shards(): jnp.dot(windows, transform_table(), preferred_element_type=jnp.float32)  5.69 us
    all_to_all x1, starting transfers between devices, shards(): lax.all_to_all(jnp.stack([slot_rows] * lax.axis_size('chan')), 'chan', 0, 0)  5.01 us
    ppermute x1, starting transfers between devices, from_behind(): return lax.ppermute(block, axis, route)  4.89 us
  transfers between devices with their start and end apart: 3, of which 2 were waited for; matrix products, arithmetic and copies ran while one was open for 21% of the time, Pallas kernels for 0%

profile of v1, /device:TPU:0, one launch (start us, length us, event | category | flops | bytes accessed | tf_op | source)
XLA Modules:
  0.0 192.4 jit_solution(9648327893744761658)
XLA Ops:
  6.5 1.1 slice.239
  7.6 4.9 %collective-permute-start = (bf16[64,2080]{1,0:T(8,128)(2,1)S(1)}, bf16[64,2080]{1,0:T(8,128)(2,1)S(1)}, u32[]{:S(2)}, u32[]{:S(2)}) collective-permute-start(bf16[64,2080]{1,0:T(8,128)(2,1)S(1)} %slice.239), channel_id=1, source_target_pairs={{0,1},{2,3},{4,5},{6,7},{8,9},{10,11},{12,13},{14,15},{16,17},{18,... | collective-permute-start | bytes 798728 | tf_op jit(solution)/shard_map/ppermute | solution.py:16
  12.5 1.0 slice_bitcast_fusion.33
  13.5 0.0 copy-start
  13.5 35.0 %cosine_convert_fusion = (bf16[4096,512]{1,0:T(8,128)(2,1)}, bf16[4096,512]{1,0:T(8,128)(2,1)}) fusion(s32[512]{0:T(512)S(1)} %iota_add_fusion), kind=kLoop, calls=%fused_computation.14 | loop fusion | flops 35651584 | bytes 8390656 | tf_op jit(solution)/shard_map/convert_element_type | solution.py:24
  48.5 0.7 fusion.51
  49.3 1.0 slice_bitcast_fusion.34
  50.3 0.0 collective-permute-done
  50.3 0.0 copy-done
  50.3 0.3 maximum_convert_fusion
  50.6 18.0 %fusion.11 = bf16[64,8192]{1,0:T(8,128)(2,1)S(1)} fusion(f32[64,8224]{1,0:T(8,128)S(1)} %maximum_convert_fusion, f32[64]{0:T(128)S(1)} %get-tuple-element.48, f32[64]{0:T(128)S(1)} %get-tuple-element.49, f32[64]{0:T(128)S(1)} %get-tuple-element.18, f32[64]{0:T(128)S(1)} %get-tuple-element.19, f32[64]{0:T(128)S(1)} %get-tuple-element.20, ...), kind=kLoop, calls=%fused_computation.23 | loop fusion | flops 34603008 | bytes 70263040 | tf_op jit(solution)/shard_map/convert_element_type | solution.py:40
  68.5 0.8 reshape.258
  69.3 1.3 fusion.58
  70.6 1.5 pad_maximum_fusion
  72.1 2.5 %reshape.259 = bf16[192,4096]{1,0:T(8,128)(2,1)} reshape(bf16[64,3,4096]{2,1,0:T(4,128)(2,1)S(1)} %pad_maximum_fusion) | data formatting | bytes 3145728 | tf_op jit(solution)/shard_map/reshape | solution.py:96
  74.6 5.7 %fusion.3 = f32[192,1024]{1,0:T(8,128)S(1)} fusion(bf16[192,4096]{1,0:T(8,128)(2,1)} %reshape.259, bf16[4096,512]{1,0:T(8,128)(2,1)} %get-tuple-element.51, bf16[4096,512]{1,0:T(8,128)(2,1)} %get-tuple-element.50), kind=kOutput, calls=%fused_computation.9 | convolution fusion | flops 1627389952 | bytes 10747904 | tf_op jit(solution)/shard_map/dot_general | solution.py:97
  80.3 0.1 fusion.57
  80.5 0.5 multiply_convert_fusion.1
  81.0 0.1 multiply_convert_fusion
  81.0 0.1 concatenate.39
  81.2 0.1 concatenate.38
  81.3 0.2 pad_maximum_fusion.1
  81.5 0.8 gather_fusion
  82.3 0.1 copy.14
  82.4 1.5 stack.2
  84.0 0.0 copy-start.2
  84.0 0.0 copy-start.1
  84.0 5.0 %all-to-all-start = ((bf16[8,36,3,1024]{3,1,2,0:T(8,128)(2,1)}), bf16[8,36,3,1024]{3,1,2,0:T(8,128)(2,1)S(1)}, u32[]{:S(2)}, u32[]{:S(2)}) async-start(bf16[8,36,3,1024]{3,1,2,0:T(8,128)(2,1)} %stack.2), calls=%async_computation | async-start | bytes 3932160 | tf_op jit(solution)/shard_map/all_to_all | solution.py:107
  89.0 0.0 reduce-scatter.2.cloned.1.call-start
  89.0 0.0 copy-done.2
  89.0 0.2 reduce-window.9
  89.2 0.0 copy-done.1
  89.2 0.1 convert_reduce_fusion
  89.3 0.7 gather_fusion.1
  90.0 0.1 concatenate.42
  90.1 0.1 concatenate.41
  90.2 0.3 maximum_convert_fusion.1
  90.5 0.2 slice_bitcast_fusion.1
  90.7 0.1 copy.17
  90.9 0.1 copy.18
  91.0 44.2 %all-to-all-done = bf16[8,36,3,1024]{3,1,2,0:T(8,128)(2,1)S(1)} async-done(((bf16[8,36,3,1024]{3,1,2,0:T(8,128)(2,1)}), bf16[8,36,3,1024]{3,1,2,0:T(8,128)(2,1)S(1)}, u32[]{:S(2)}, u32[]{:S(2)}) %all-to-all-start) | async-done | bytes 1769504 | tf_op jit(solution)/shard_map/all_to_all | solution.py:107
  135.2 2.9 %copy.19 = bf16[8,36,3,1024]{3,2,1,0:T(4,128)(2,1)} copy(bf16[8,36,3,1024]{3,1,2,0:T(8,128)(2,1)S(1)} %all-to-all-done) | data formatting | bytes 3538944 | tf_op jit(solution)/shard_map/reshape | solution.py:106
  138.1 2.3 %gather_fusion.2 = bf16[12,3,1024]{2,1,0:T(4,128)(2,1)S(1)} fusion(bf16[288,3,1024]{2,1,0:T(4,128)(2,1)} %bitcast.96, s32[1024]{0:T(1024)S(1)} %pad_clamp_fusion), kind=kCustom, calls=%fused_computation.2 | custom fusion | bytes 147504 | tf_op jit(solution)/shard_map/gather | solution.py:109
  140.4 1.4 add_reduce_fusion
  141.9 2.1 %maximum_multiply_fusion = f32[64,12,1024]{2,0,1:T(8,128)} fusion(f32[64,12,512]{2,0,1:T(8,128)S(1)} %get-tuple-element.6, f32[64,12,512]{2,0,1:T(8,128)S(1)} %get-tuple-element.5), kind=kLoop, calls=%fused_computation.20 | loop fusion | flops 1572864 | bytes 6291456 | tf_op jit(solution)/shard_map/mul | solution.py:76
  144.0 0.0 reduce-scatter.2.cloned.1.call-update
  144.0 41.6 %reduce-scatter.2.cloned.1.call-done = f32[32,12,1024]{2,0,1:T(8,128)} async-done(((f32[64,12,1024]{2,0,1:T(8,128)}), f32[32,12,1024]{2,0,1:T(8,128)}) %reduce-scatter.2.cloned.1.call-update) | async-done | bytes 1572880 | tf_op jit(solution)/shard_map/reduce_scatter | solution.py:117
  (9 shorter events, 0.1 us)
Async XLA Ops:
  7.6 42.6 %collective-permute-start = (bf16[64,2080]{1,0:T(8,128)(2,1)S(1)}, bf16[64,2080]{1,0:T(8,128)(2,1)S(1)}, u32[]{:S(2)}, u32[]{:S(2)}) collective-permute-start(bf16[64,2080]{1,0:T(8,128)(2,1)S(1)} %slice.239), channel_id=1, source_target_pairs={{0,1},{2,3},{4,5},{6,7},{8,9},{10,11},{12,13},{14,15},{16,17},{18,... | collective-permute-start | bytes 798728 | tf_op jit(solution)/shard_map/ppermute | solution.py:16
  13.5 36.8 %copy-start = (bf16[64,6144]{1,0:T(8,128)(2,1)S(1)}, bf16[64,6144]{1,0:T(8,128)(2,1)}, u32[]{:S(2)}) copy-start(bf16[64,6144]{1,0:T(8,128)(2,1)} %param.5) | copy-start | bytes 2359300
  84.0 5.1 %copy-start.2 = (s32[8]{0:T(128)S(1)}, s32[8]{0:T(128)}, u32[]{:S(2)}) copy-start(s32[8]{0:T(128)} %param.7) | copy-start | bytes 100
  84.0 5.3 %copy-start.1 = (s32[1,12]{1,0:T(1,128)S(1)}, s32[1,12]{1,0:T(1,128)}, u32[]{:S(2)}) copy-start(s32[1,12]{1,0:T(1,128)} %param.9) | copy-start | bytes 148
  84.0 51.2 %all-to-all-start = ((bf16[8,36,3,1024]{3,1,2,0:T(8,128)(2,1)}), bf16[8,36,3,1024]{3,1,2,0:T(8,128)(2,1)S(1)}, u32[]{:S(2)}, u32[]{:S(2)}) async-start(bf16[8,36,3,1024]{3,1,2,0:T(8,128)(2,1)} %stack.2), calls=%async_computation | async-start | bytes 3932160 | tf_op jit(solution)/shard_map/all_to_all | solution.py:107
  89.0 96.6 %reduce-scatter.2.cloned.1.call-start = ((), (), s32[]{:S(2)}) async-start(), calls=%async_computation.2 | async-start | bytes 4718592 | tf_op jit(solution)/shard_map/reduce_scatter | solution.py:117
Sparse Core Ops, SparseCore 0:
  144.1 41.4 reduce-scatter.1
